TPU v7x, 128 devices: a whole 4x4x4 slice. The times are simulated.
128 devices in a mesh: ctx: 32 (over y, x, z_lo), batch: 4 (over z_hi, core).
Axes of the slice: x: 4, y: 4, z: 4 (z_hi: 2, z_lo: 2; z = z_hi * 2 + z_lo), core: 2. Of those that a mesh axis runs over, the one named last changes fastest.
Arguments:
- queries: bfloat16 [4, 8192, 2048], P('batch', 'ctx'), may hold values from -120 to 120
- keys: bfloat16 [4, 8192, 512], P('batch', 'ctx'), may hold values from -6 to 6
- values: bfloat16 [4, 8192, 512], P('batch', 'ctx'), may hold values from -6 to 6
- tau: float32 [16], replicated, may hold values from 0.5 to 2
- out_grad: bfloat16 [4, 8192, 2048], P('batch', 'ctx'), may hold values from -18 to 18
- key_blocks: int32 [4, 64, 13], replicated, may hold values from 0 to 63, as said below
Outputs:
- attended: bfloat16 [4, 8192, 2048], P('batch', 'ctx')
- query_grad: bfloat16 [4, 8192, 2048], P('batch', 'ctx')
- key_grad: bfloat16 [4, 8192, 512], P('batch', 'ctx')
- value_grad: bfloat16 [4, 8192, 512], P('batch', 'ctx')
- tau_grad: float32 [16], replicated
Inputs may be any that keep to these rules, and one draw needn't show every extreme that they name: `key_blocks`: row a of head group g lists a - 1, a, a + 1, then a + m s and a - m s for m = 1 to 5, all modulo 64, with a stride s of 2 or 3 drawn for each group and row.
All inputs are finite; a program needn't handle non-finite values.
Results may differ from a plain program's by a relative error of at most 0.0051.
Values may be sent and summed in bfloat16 or wider, within the bound.
A program may use at most 192 MiB of HBM per device.

v0:
```python
import math
import jax
import jax.numpy as jnp
from jax import lax
from jax.sharding import PartitionSpec as P

HEADS = 16
KV_HEADS = 4
HD = 128
BLOCK = 128


def passed_along(block, axis, distance):
    devices = range(lax.axis_size(axis))
    route = [((i - distance) % len(devices), i) for i in devices]
    return lax.ppermute(block, axis, route)


def body(queries, keys, values, tau, out_grad, key_blocks):
    ctx_size = lax.axis_size("ctx")
    myself = lax.axis_index("ctx")
    tokens = queries.shape[1]
    local_blocks = tokens // BLOCK
    listed_count = key_blocks.shape[2]
    block_reach = 3 * ((listed_count - 3) // 2)
    reach_dev = min((local_blocks - 1 + block_reach) // local_blocks, ctx_size // 2)
    slot_count = 2 * reach_dev + 1
    per_group = HEADS // KV_HEADS
    root_hd = math.sqrt(HD)
    paired = jnp.stack([keys[0], values[0]])
    window = jnp.zeros((2, slot_count, tokens, KV_HEADS * HD), jnp.bfloat16)
    farthest = passed_along(paired, "ctx", -reach_dev)
    window = lax.dynamic_update_slice_in_dim(window, farthest[:, None], slot_count - 1, 1)

    def walk_turn(turn_no, state_in):
        current, filled = state_in
        current = passed_along(current, "ctx", 1)
        filled = lax.dynamic_update_slice_in_dim(
            filled, current[:, None], slot_count - 1 - turn_no, 1
        )
        return (current, filled)

    window = lax.fori_loop(1, slot_count, walk_turn, (farthest, window))[1]
    blocks_all = window.reshape(2, slot_count * local_blocks, BLOCK, KV_HEADS, HD)
    own_lists = lax.dynamic_slice_in_dim(key_blocks, myself * local_blocks, local_blocks, 1)
    window_index = (
        own_lists // local_blocks - myself + reach_dev
    ) % ctx_size * local_blocks + own_lists % local_blocks
    window_ids = jnp.arange(slot_count * local_blocks, dtype=jnp.int32)
    query_all = queries[0].reshape(local_blocks, BLOCK, KV_HEADS, per_group, HD)
    grad_all = out_grad[0].reshape(local_blocks, BLOCK, KV_HEADS, per_group, HD)
    factor = tau.reshape(KV_HEADS, per_group) / root_hd
    results = []
    query_parts = []
    placed_parts = []
    scale_parts = []
    for group_id in range(KV_HEADS):
        picks = window_index[group_id].reshape(-1)
        key_rows = jnp.take(blocks_all[0, :, :, group_id], picks, axis=0).reshape(
            local_blocks, listed_count * BLOCK, HD
        )
        value_rows = jnp.take(blocks_all[1, :, :, group_id], picks, axis=0).reshape(
            local_blocks, listed_count * BLOCK, HD
        )
        query_rows = query_all[:, :, group_id]
        grad_rows = grad_all[:, :, group_id]
        scale_row = factor[group_id]
        raw_scores = jnp.einsum(
            "nqhd,nkd->nhqk", query_rows, key_rows, preferred_element_type=jnp.float32
        )
        weights = jax.nn.softmax(raw_scores * scale_row[None, :, None, None], axis=-1)
        probs_low = weights.astype(jnp.bfloat16)
        result = jnp.einsum(
            "nhqk,nkd->nqhd", probs_low, value_rows, preferred_element_type=jnp.float32
        )
        row_dot = jnp.sum(grad_rows.astype(jnp.float32) * result, axis=-1)
        dweights = jnp.einsum(
            "nqhd,nkd->nhqk", grad_rows, value_rows, preferred_element_type=jnp.float32
        )
        dscores = weights * (dweights - row_dot.transpose(0, 2, 1)[..., None])
        scale_parts.append(jnp.sum(dscores * raw_scores, axis=(0, 2, 3)) / root_hd)
        scaled = (dscores * scale_row[None, :, None, None]).astype(jnp.bfloat16)
        query_part = jnp.einsum(
            "nhqk,nkd->nqhd", scaled, key_rows, preferred_element_type=jnp.float32
        )
        key_part = jnp.einsum(
            "nhqk,nqhd->nkd", scaled, query_rows, preferred_element_type=jnp.float32
        )
        value_part = jnp.einsum(
            "nhqk,nqhd->nkd", probs_low, grad_rows, preferred_element_type=jnp.float32
        )
        chooser = (picks[:, None] == window_ids[None, :]).astype(jnp.float32)
        both_parts = jnp.stack([key_part, value_part]).reshape(
            2, local_blocks * listed_count, BLOCK * HD
        )
        placed_parts.append(
            jnp.einsum("sw,csx->cwx", chooser, both_parts, precision=lax.Precision.HIGHEST)
        )
        results.append(result)
        query_parts.append(query_part)
    attended = jnp.stack(results, axis=2).reshape(1, tokens, HEADS * HD).astype(jnp.bfloat16)
    query_grad = jnp.stack(query_parts, axis=2).reshape(1, tokens, HEADS * HD).astype(jnp.bfloat16)
    stacked = jnp.stack(placed_parts).reshape(KV_HEADS, 2, slot_count, local_blocks, BLOCK, HD)
    grads_window = stacked.transpose(2, 1, 3, 4, 0, 5).reshape(slot_count, 2, tokens, KV_HEADS * HD)

    def chain_turn(turn_no, partial_sum):
        moved = passed_along(partial_sum, "ctx", -1)
        return moved + lax.dynamic_index_in_dim(grads_window, turn_no, 0, keepdims=False)

    partial_sum = lax.fori_loop(1, slot_count, chain_turn, grads_window[0])
    summed = passed_along(partial_sum.astype(jnp.bfloat16), "ctx", reach_dev).astype(
        partial_sum.dtype
    )
    key_grad = summed[0].reshape(1, tokens, KV_HEADS * HD).astype(jnp.bfloat16)
    value_grad = summed[1].reshape(1, tokens, KV_HEADS * HD).astype(jnp.bfloat16)
    scale_total = lax.psum(jnp.stack(scale_parts), ("ctx", "batch"))
    tau_grad = scale_total.reshape(HEADS) / math.sqrt(lax.axis_size("batch") * ctx_size * tokens)
    return (attended, query_grad, key_grad, value_grad, tau_grad)


def solution(mesh):
    return jax.shard_map(
        body,
        mesh=mesh,
        in_specs=(
            P("batch", "ctx", None),
            P("batch", "ctx", None),
            P("batch", "ctx", None),
            P(),
            P("batch", "ctx", None),
            P(),
        ),
        out_specs=(
            P("batch", "ctx", None),
            P("batch", "ctx", None),
            P("batch", "ctx", None),
            P("batch", "ctx", None),
            P(),
        ),
        check_vma=False,
    )
```

profile of v0, /device:TPU:0, one launch (start us, length us, event | category | flops | bytes accessed | tf_op | source)
XLA Modules:
  0.0 1086.7 jit_solution(6687766181752277367)
XLA Ops:
  17.2 5.5 dynamic_update_slice.10
  22.7 280.8 %while.30 = (s32[]{:T(128)}, bf16[2,256,512]{2,1,0:T(8,128)(2,1)}, bf16[2,17,256,512]{3,2,0,1:T(8,128)(2,1)}, s32[]{:T(128)}, s32[]{:T(128)}, /*index=5*/s32[]{:T(128)}, s32[]{:T(128)}) while((s32[]{:T(128)}, bf16[2,256,512]{2,1,0:T(8,128)(2,1)}, bf16[2,17,256,512]{3,2,0,1:T(8,128)(2,1)}, s32[]{:T(128)}, s32[]{:T(128)}, /*index=5*/s32[]{:T(128)}, ...), condition=%wide.region_1.0_spmd, body=%wide.region_0.0_spmd.sunk | while | flops 6 | bytes 4194471 | solution.py:43
  24.7 16.6 %collective-permute-done = bf16[2,256,512]{2,1,0:T(8,128)(2,1)S(1)} collective-permute-done((bf16[2,256,512]{2,1,0:T(8,128)(2,1)}, bf16[2,256,512]{2,1,0:T(8,128)(2,1)S(1)}, u32[]{:S(2)}, u32[]{:S(2)}) %collective-permute-start) | collective-permute-done | bytes 524320 | tf_op jit(solution)/shard_map/while/body/eval_jaxpr/ppermute | solution.py:16
  42.9 16.6 %collective-permute-done = bf16[2,256,512]{2,1,0:T(8,128)(2,1)S(1)} collective-permute-done((bf16[2,256,512]{2,1,0:T(8,128)(2,1)}, bf16[2,256,512]{2,1,0:T(8,128)(2,1)S(1)}, u32[]{:S(2)}, u32[]{:S(2)}) %collective-permute-start) | collective-permute-done | bytes 524320 | tf_op jit(solution)/shard_map/while/body/eval_jaxpr/ppermute | solution.py:16
  61.2 15.7 %collective-permute-done = bf16[2,256,512]{2,1,0:T(8,128)(2,1)S(1)} collective-permute-done((bf16[2,256,512]{2,1,0:T(8,128)(2,1)}, bf16[2,256,512]{2,1,0:T(8,128)(2,1)S(1)}, u32[]{:S(2)}, u32[]{:S(2)}) %collective-permute-start) | collective-permute-done | bytes 524320 | tf_op jit(solution)/shard_map/while/body/eval_jaxpr/ppermute | solution.py:16
  78.5 14.7 %collective-permute-done = bf16[2,256,512]{2,1,0:T(8,128)(2,1)S(1)} collective-permute-done((bf16[2,256,512]{2,1,0:T(8,128)(2,1)}, bf16[2,256,512]{2,1,0:T(8,128)(2,1)S(1)}, u32[]{:S(2)}, u32[]{:S(2)}) %collective-permute-start) | collective-permute-done | bytes 524320 | tf_op jit(solution)/shard_map/while/body/eval_jaxpr/ppermute | solution.py:16
  94.8 13.8 %collective-permute-done = bf16[2,256,512]{2,1,0:T(8,128)(2,1)S(1)} collective-permute-done((bf16[2,256,512]{2,1,0:T(8,128)(2,1)}, bf16[2,256,512]{2,1,0:T(8,128)(2,1)S(1)}, u32[]{:S(2)}, u32[]{:S(2)}) %collective-permute-start) | collective-permute-done | bytes 524320 | tf_op jit(solution)/shard_map/while/body/eval_jaxpr/ppermute | solution.py:16
  110.3 13.6 %collective-permute-done = bf16[2,256,512]{2,1,0:T(8,128)(2,1)S(1)} collective-permute-done((bf16[2,256,512]{2,1,0:T(8,128)(2,1)}, bf16[2,256,512]{2,1,0:T(8,128)(2,1)S(1)}, u32[]{:S(2)}, u32[]{:S(2)}) %collective-permute-start) | collective-permute-done | bytes 524320 | tf_op jit(solution)/shard_map/while/body/eval_jaxpr/ppermute | solution.py:16
  125.5 13.6 %collective-permute-done = bf16[2,256,512]{2,1,0:T(8,128)(2,1)S(1)} collective-permute-done((bf16[2,256,512]{2,1,0:T(8,128)(2,1)}, bf16[2,256,512]{2,1,0:T(8,128)(2,1)S(1)}, u32[]{:S(2)}, u32[]{:S(2)}) %collective-permute-start) | collective-permute-done | bytes 524320 | tf_op jit(solution)/shard_map/while/body/eval_jaxpr/ppermute | solution.py:16
  140.8 13.7 %collective-permute-done = bf16[2,256,512]{2,1,0:T(8,128)(2,1)S(1)} collective-permute-done((bf16[2,256,512]{2,1,0:T(8,128)(2,1)}, bf16[2,256,512]{2,1,0:T(8,128)(2,1)S(1)}, u32[]{:S(2)}, u32[]{:S(2)}) %collective-permute-start) | collective-permute-done | bytes 524320 | tf_op jit(solution)/shard_map/while/body/eval_jaxpr/ppermute | solution.py:16
  156.1 14.8 %collective-permute-done = bf16[2,256,512]{2,1,0:T(8,128)(2,1)S(1)} collective-permute-done((bf16[2,256,512]{2,1,0:T(8,128)(2,1)}, bf16[2,256,512]{2,1,0:T(8,128)(2,1)S(1)}, u32[]{:S(2)}, u32[]{:S(2)}) %collective-permute-start) | collective-permute-done | bytes 524320 | tf_op jit(solution)/shard_map/while/body/eval_jaxpr/ppermute | solution.py:16
  172.5 15.9 %collective-permute-done = bf16[2,256,512]{2,1,0:T(8,128)(2,1)S(1)} collective-permute-done((bf16[2,256,512]{2,1,0:T(8,128)(2,1)}, bf16[2,256,512]{2,1,0:T(8,128)(2,1)S(1)}, u32[]{:S(2)}, u32[]{:S(2)}) %collective-permute-start) | collective-permute-done | bytes 524320 | tf_op jit(solution)/shard_map/while/body/eval_jaxpr/ppermute | solution.py:16
  190.0 17.0 %collective-permute-done = bf16[2,256,512]{2,1,0:T(8,128)(2,1)S(1)} collective-permute-done((bf16[2,256,512]{2,1,0:T(8,128)(2,1)}, bf16[2,256,512]{2,1,0:T(8,128)(2,1)S(1)}, u32[]{:S(2)}, u32[]{:S(2)}) %collective-permute-start) | collective-permute-done | bytes 524320 | tf_op jit(solution)/shard_map/while/body/eval_jaxpr/ppermute | solution.py:16
  208.6 18.1 %collective-permute-done = bf16[2,256,512]{2,1,0:T(8,128)(2,1)S(1)} collective-permute-done((bf16[2,256,512]{2,1,0:T(8,128)(2,1)}, bf16[2,256,512]{2,1,0:T(8,128)(2,1)S(1)}, u32[]{:S(2)}, u32[]{:S(2)}) %collective-permute-start) | collective-permute-done | bytes 524320 | tf_op jit(solution)/shard_map/while/body/eval_jaxpr/ppermute | solution.py:16
  228.3 19.2 %collective-permute-done = bf16[2,256,512]{2,1,0:T(8,128)(2,1)S(1)} collective-permute-done((bf16[2,256,512]{2,1,0:T(8,128)(2,1)}, bf16[2,256,512]{2,1,0:T(8,128)(2,1)S(1)}, u32[]{:S(2)}, u32[]{:S(2)}) %collective-permute-start) | collective-permute-done | bytes 524320 | tf_op jit(solution)/shard_map/while/body/eval_jaxpr/ppermute | solution.py:16
  249.1 18.4 %collective-permute-done = bf16[2,256,512]{2,1,0:T(8,128)(2,1)S(1)} collective-permute-done((bf16[2,256,512]{2,1,0:T(8,128)(2,1)}, bf16[2,256,512]{2,1,0:T(8,128)(2,1)S(1)}, u32[]{:S(2)}, u32[]{:S(2)}) %collective-permute-start) | collective-permute-done | bytes 524320 | tf_op jit(solution)/shard_map/while/body/eval_jaxpr/ppermute | solution.py:16
  269.1 17.5 %collective-permute-done = bf16[2,256,512]{2,1,0:T(8,128)(2,1)S(1)} collective-permute-done((bf16[2,256,512]{2,1,0:T(8,128)(2,1)}, bf16[2,256,512]{2,1,0:T(8,128)(2,1)S(1)}, u32[]{:S(2)}, u32[]{:S(2)}) %collective-permute-start) | collective-permute-done | bytes 524320 | tf_op jit(solution)/shard_map/while/body/eval_jaxpr/ppermute | solution.py:16
  288.3 13.6 %collective-permute-done = bf16[2,256,512]{2,1,0:T(8,128)(2,1)S(1)} collective-permute-done((bf16[2,256,512]{2,1,0:T(8,128)(2,1)}, bf16[2,256,512]{2,1,0:T(8,128)(2,1)S(1)}, u32[]{:S(2)}, u32[]{:S(2)}) %collective-permute-start) | collective-permute-done | bytes 524320 | tf_op jit(solution)/shard_map/while/body/eval_jaxpr/ppermute | solution.py:16
  303.5 8.0 copy.85
  311.5 13.3 %reshape.174 = bf16[2,34,128,4,128]{4,3,2,1,0:T(4,128)(2,1)} reshape(bf16[2,17,256,512]{3,2,1,0:T(8,128)(2,1)} %copy.85) | data formatting | bytes 17825792 | tf_op jit(solution)/shard_map/reshape | solution.py:44
  324.9 23.1 %fusion.82 = (bf16[1,34,128,1,128]{4,3,2,1,0:T(2,128)(2,1)S(1)}, bf16[1,34,128,1,128]{4,3,2,1,0:T(2,128)(2,1)}, bf16[1,34,128,1,128]{4,3,2,1,0:T(2,128)(2,1)}, b...) fusion(bf16[2,34,128,4,128]{4,3,2,1,0:T(4,128)(2,1)} %reshape.174), kind=kLoop, calls=%fused_computation.196 | loop fusion | bytes 17825792 | tf_op jit(solution)/shard_map/slice | solution.py:59
  390.2 4.9 fusion.58
  424.4 4.9 fusion.59
  459.8 6.5 convolution_bitcast_fusion.2
  474.9 6.5 convolution_bitcast_fusion.1
  513.1 4.9 convolution_bitcast_fusion
  522.3 63.8 %psum.7 = f32[4,4]{1,0:T(4,128)S(1)} all-reduce(f32[4,4]{1,0:T(4,128)S(1)} %pad_maximum_fusion.3), channel_id=1, replica_groups=mesh['ctx'=32,'batch'=4] {'ctx','batch'}, use_global_device_ids=true, to_apply=%region_20.22 | all-reduce | flops 16 | bytes 128 | tf_op jit(solution)/shard_map/psum | solution.py:116
  588.4 5.2 convolution_bitcast_fusion.11
  596.3 6.5 convolution_bitcast_fusion.3
  614.7 6.9 copy.256
  621.6 20.0 %copy.128 = f32[17,2,2,128,4,128]{5,4,3,2,1,0:T(4,128)} copy(f32[17,2,2,128,4,128]{5,3,2,0,1,4:T(8,128)S(1)} %bitcast.371) | data formatting | bytes 35651584 | tf_op jit(solution)/shard_map/transpose | solution.py:104
  641.6 21.9 %reshape.183 = f32[17,2,256,512]{3,2,1,0:T(8,128)} reshape(f32[17,2,2,128,4,128]{5,4,3,2,1,0:T(4,128)} %copy.128) | data formatting | bytes 35651584 | tf_op jit(solution)/shard_map/reshape | solution.py:104
  665.9 406.7 %while.31 = (s32[]{:T(128)}, f32[2,256,512]{2,1,0:T(8,128)S(1)}, f32[17,2,256,512]{3,2,1,0:T(8,128)}, s32[]{:T(128)}, s32[]{:T(128)}, /*index=5*/s32[]{:T(128)}) while((s32[]{:T(128)}, f32[2,256,512]{2,1,0:T(8,128)S(1)}, f32[17,2,256,512]{3,2,1,0:T(8,128)}, s32[]{:T(128)}, s32[]{:T(128)}, /*index=5*/s32[]{:T(128)}) %tuple.109), condition=%wide.region_15.17_spmd, body=%wide.region_14.16_spmd.sunk | while | flops 262149 | bytes 7340179 | solution.py:110
  666.8 23.6 %collective-permute-done.1 = f32[2,256,512]{2,1,0:T(8,128)S(1)} collective-permute-done((f32[2,256,512]{2,1,0:T(8,128)S(1)}, f32[2,256,512]{2,1,0:T(8,128)S(1)}, u32[]{:S(2)}, u32[]{:S(2)}) %collective-permute-start.1) | collective-permute-done | bytes 1048608 | tf_op jit(solution)/shard_map/while/body/eval_jaxpr/ppermute | solution.py:16
  691.9 6.0 collective-permute-start.1
  697.9 22.1 %collective-permute-done.1 = f32[2,256,512]{2,1,0:T(8,128)S(1)} collective-permute-done((f32[2,256,512]{2,1,0:T(8,128)S(1)}, f32[2,256,512]{2,1,0:T(8,128)S(1)}, u32[]{:S(2)}, u32[]{:S(2)}) %collective-permute-start.1) | collective-permute-done | bytes 1048608 | tf_op jit(solution)/shard_map/while/body/eval_jaxpr/ppermute | solution.py:16
  721.4 6.8 collective-permute-start.1
  728.2 21.2 %collective-permute-done.1 = f32[2,256,512]{2,1,0:T(8,128)S(1)} collective-permute-done((f32[2,256,512]{2,1,0:T(8,128)S(1)}, f32[2,256,512]{2,1,0:T(8,128)S(1)}, u32[]{:S(2)}, u32[]{:S(2)}) %collective-permute-start.1) | collective-permute-done | bytes 1048608 | tf_op jit(solution)/shard_map/while/body/eval_jaxpr/ppermute | solution.py:16
  750.8 6.8 collective-permute-start.1
  757.5 20.2 %collective-permute-done.1 = f32[2,256,512]{2,1,0:T(8,128)S(1)} collective-permute-done((f32[2,256,512]{2,1,0:T(8,128)S(1)}, f32[2,256,512]{2,1,0:T(8,128)S(1)}, u32[]{:S(2)}, u32[]{:S(2)}) %collective-permute-start.1) | collective-permute-done | bytes 1048608 | tf_op jit(solution)/shard_map/while/body/eval_jaxpr/ppermute | solution.py:16
  779.2 6.8 collective-permute-start.1
  786.0 19.3 %collective-permute-done.1 = f32[2,256,512]{2,1,0:T(8,128)S(1)} collective-permute-done((f32[2,256,512]{2,1,0:T(8,128)S(1)}, f32[2,256,512]{2,1,0:T(8,128)S(1)}, u32[]{:S(2)}, u32[]{:S(2)}) %collective-permute-start.1) | collective-permute-done | bytes 1048608 | tf_op jit(solution)/shard_map/while/body/eval_jaxpr/ppermute | solution.py:16
  806.7 6.8 collective-permute-start.1
  813.5 18.4 %collective-permute-done.1 = f32[2,256,512]{2,1,0:T(8,128)S(1)} collective-permute-done((f32[2,256,512]{2,1,0:T(8,128)S(1)}, f32[2,256,512]{2,1,0:T(8,128)S(1)}, u32[]{:S(2)}, u32[]{:S(2)}) %collective-permute-start.1) | collective-permute-done | bytes 1048608 | tf_op jit(solution)/shard_map/while/body/eval_jaxpr/ppermute | solution.py:16
  833.3 6.8 collective-permute-start.1
  840.1 17.5 %collective-permute-done.1 = f32[2,256,512]{2,1,0:T(8,128)S(1)} collective-permute-done((f32[2,256,512]{2,1,0:T(8,128)S(1)}, f32[2,256,512]{2,1,0:T(8,128)S(1)}, u32[]{:S(2)}, u32[]{:S(2)}) %collective-permute-start.1) | collective-permute-done | bytes 1048608 | tf_op jit(solution)/shard_map/while/body/eval_jaxpr/ppermute | solution.py:16
  859.0 6.8 collective-permute-start.1
  865.8 16.5 %collective-permute-done.1 = f32[2,256,512]{2,1,0:T(8,128)S(1)} collective-permute-done((f32[2,256,512]{2,1,0:T(8,128)S(1)}, f32[2,256,512]{2,1,0:T(8,128)S(1)}, u32[]{:S(2)}, u32[]{:S(2)}) %collective-permute-start.1) | collective-permute-done | bytes 1048608 | tf_op jit(solution)/shard_map/while/body/eval_jaxpr/ppermute | solution.py:16
  883.8 6.8 collective-permute-start.1
  890.5 15.6 %collective-permute-done.1 = f32[2,256,512]{2,1,0:T(8,128)S(1)} collective-permute-done((f32[2,256,512]{2,1,0:T(8,128)S(1)}, f32[2,256,512]{2,1,0:T(8,128)S(1)}, u32[]{:S(2)}, u32[]{:S(2)}) %collective-permute-start.1) | collective-permute-done | bytes 1048608 | tf_op jit(solution)/shard_map/while/body/eval_jaxpr/ppermute | solution.py:16
  907.6 6.8 collective-permute-start.1
  914.4 15.1 %collective-permute-done.1 = f32[2,256,512]{2,1,0:T(8,128)S(1)} collective-permute-done((f32[2,256,512]{2,1,0:T(8,128)S(1)}, f32[2,256,512]{2,1,0:T(8,128)S(1)}, u32[]{:S(2)}, u32[]{:S(2)}) %collective-permute-start.1) | collective-permute-done | bytes 1048608 | tf_op jit(solution)/shard_map/while/body/eval_jaxpr/ppermute | solution.py:16
  930.9 6.8 collective-permute-start.1
  937.7 15.1 %collective-permute-done.1 = f32[2,256,512]{2,1,0:T(8,128)S(1)} collective-permute-done((f32[2,256,512]{2,1,0:T(8,128)S(1)}, f32[2,256,512]{2,1,0:T(8,128)S(1)}, u32[]{:S(2)}, u32[]{:S(2)}) %collective-permute-start.1) | collective-permute-done | bytes 1048608 | tf_op jit(solution)/shard_map/while/body/eval_jaxpr/ppermute | solution.py:16
  954.3 6.8 collective-permute-start.1
  961.0 15.1 %collective-permute-done.1 = f32[2,256,512]{2,1,0:T(8,128)S(1)} collective-permute-done((f32[2,256,512]{2,1,0:T(8,128)S(1)}, f32[2,256,512]{2,1,0:T(8,128)S(1)}, u32[]{:S(2)}, u32[]{:S(2)}) %collective-permute-start.1) | collective-permute-done | bytes 1048608 | tf_op jit(solution)/shard_map/while/body/eval_jaxpr/ppermute | solution.py:16
  977.6 6.8 collective-permute-start.1
  984.4 15.5 %collective-permute-done.1 = f32[2,256,512]{2,1,0:T(8,128)S(1)} collective-permute-done((f32[2,256,512]{2,1,0:T(8,128)S(1)}, f32[2,256,512]{2,1,0:T(8,128)S(1)}, u32[]{:S(2)}, u32[]{:S(2)}) %collective-permute-start.1) | collective-permute-done | bytes 1048608 | tf_op jit(solution)/shard_map/while/body/eval_jaxpr/ppermute | solution.py:16
  1001.3 6.8 collective-permute-start.1
  1008.1 16.6 %collective-permute-done.1 = f32[2,256,512]{2,1,0:T(8,128)S(1)} collective-permute-done((f32[2,256,512]{2,1,0:T(8,128)S(1)}, f32[2,256,512]{2,1,0:T(8,128)S(1)}, u32[]{:S(2)}, u32[]{:S(2)}) %collective-permute-start.1) | collective-permute-done | bytes 1048608 | tf_op jit(solution)/shard_map/while/body/eval_jaxpr/ppermute | solution.py:16
  1026.1 6.8 collective-permute-start.1
  1032.9 17.7 %collective-permute-done.1 = f32[2,256,512]{2,1,0:T(8,128)S(1)} collective-permute-done((f32[2,256,512]{2,1,0:T(8,128)S(1)}, f32[2,256,512]{2,1,0:T(8,128)S(1)}, u32[]{:S(2)}, u32[]{:S(2)}) %collective-permute-start.1) | collective-permute-done | bytes 1048608 | tf_op jit(solution)/shard_map/while/body/eval_jaxpr/ppermute | solution.py:16
  1052.0 6.8 collective-permute-start.1
  1058.8 12.3 %collective-permute-done.1 = f32[2,256,512]{2,1,0:T(8,128)S(1)} collective-permute-done((f32[2,256,512]{2,1,0:T(8,128)S(1)}, f32[2,256,512]{2,1,0:T(8,128)S(1)}, u32[]{:S(2)}, u32[]{:S(2)}) %collective-permute-start.1) | collective-permute-done | bytes 1048608 | tf_op jit(solution)/shard_map/while/body/eval_jaxpr/ppermute | solution.py:16
  (289 shorter events, 247.5 us)
Async XLA Ops:
  0.6 10.7 copy-start.18
  2.6 14.6 %collective-permute-start.2 = (bf16[2,256,512]{2,1,0:T(8,128)(2,1)}, bf16[2,256,512]{2,1,0:T(8,128)(2,1)}, u32[]{:S(2)}, u32[]{:S(2)}) collective-permute-start(bf16[2,256,512]{2,1,0:T(8,128)(2,1)} %pad_maximum_fusion.2), channel_id=1, source_target_pairs={{32,0},{36,4},{40,8},{44,12},{48,16},{52,20},{56,24},{60,28},{64,3... | collective-permute-start | bytes 1572872 | tf_op jit(solution)/shard_map/ppermute | solution.py:16
  22.7 18.5 %collective-permute-start = (bf16[2,256,512]{2,1,0:T(8,128)(2,1)}, bf16[2,256,512]{2,1,0:T(8,128)(2,1)S(1)}, u32[]{:S(2)}, u32[]{:S(2)}) collective-permute-start(bf16[2,256,512]{2,1,0:T(8,128)(2,1)} %get-tuple-element.288), channel_id=1, source_target_pairs={{124,0},{0,4},{4,8},{8,12},{12,16},{16,20},{20,24},{24,28},{28,32}... | collective-permute-start | bytes 1572872 | tf_op jit(solution)/shard_map/while/body/eval_jaxpr/ppermute | solution.py:16
  42.9 16.6 %collective-permute-start = (bf16[2,256,512]{2,1,0:T(8,128)(2,1)}, bf16[2,256,512]{2,1,0:T(8,128)(2,1)S(1)}, u32[]{:S(2)}, u32[]{:S(2)}) collective-permute-start(bf16[2,256,512]{2,1,0:T(8,128)(2,1)} %get-tuple-element.288), channel_id=1, source_target_pairs={{124,0},{0,4},{4,8},{8,12},{12,16},{16,20},{20,24},{24,28},{28,32}... | collective-permute-start | bytes 1572872 | tf_op jit(solution)/shard_map/while/body/eval_jaxpr/ppermute | solution.py:16
  61.2 15.7 %collective-permute-start = (bf16[2,256,512]{2,1,0:T(8,128)(2,1)}, bf16[2,256,512]{2,1,0:T(8,128)(2,1)S(1)}, u32[]{:S(2)}, u32[]{:S(2)}) collective-permute-start(bf16[2,256,512]{2,1,0:T(8,128)(2,1)} %get-tuple-element.288), channel_id=1, source_target_pairs={{124,0},{0,4},{4,8},{8,12},{12,16},{16,20},{20,24},{24,28},{28,32}... | collective-permute-start | bytes 1572872 | tf_op jit(solution)/shard_map/while/body/eval_jaxpr/ppermute | solution.py:16
  78.5 14.7 %collective-permute-start = (bf16[2,256,512]{2,1,0:T(8,128)(2,1)}, bf16[2,256,512]{2,1,0:T(8,128)(2,1)S(1)}, u32[]{:S(2)}, u32[]{:S(2)}) collective-permute-start(bf16[2,256,512]{2,1,0:T(8,128)(2,1)} %get-tuple-element.288), channel_id=1, source_target_pairs={{124,0},{0,4},{4,8},{8,12},{12,16},{16,20},{20,24},{24,28},{28,32}... | collective-permute-start | bytes 1572872 | tf_op jit(solution)/shard_map/while/body/eval_jaxpr/ppermute | solution.py:16
  94.8 13.8 %collective-permute-start = (bf16[2,256,512]{2,1,0:T(8,128)(2,1)}, bf16[2,256,512]{2,1,0:T(8,128)(2,1)S(1)}, u32[]{:S(2)}, u32[]{:S(2)}) collective-permute-start(bf16[2,256,512]{2,1,0:T(8,128)(2,1)} %get-tuple-element.288), channel_id=1, source_target_pairs={{124,0},{0,4},{4,8},{8,12},{12,16},{16,20},{20,24},{24,28},{28,32}... | collective-permute-start | bytes 1572872 | tf_op jit(solution)/shard_map/while/body/eval_jaxpr/ppermute | solution.py:16
  110.3 13.6 %collective-permute-start = (bf16[2,256,512]{2,1,0:T(8,128)(2,1)}, bf16[2,256,512]{2,1,0:T(8,128)(2,1)S(1)}, u32[]{:S(2)}, u32[]{:S(2)}) collective-permute-start(bf16[2,256,512]{2,1,0:T(8,128)(2,1)} %get-tuple-element.288), channel_id=1, source_target_pairs={{124,0},{0,4},{4,8},{8,12},{12,16},{16,20},{20,24},{24,28},{28,32}... | collective-permute-start | bytes 1572872 | tf_op jit(solution)/shard_map/while/body/eval_jaxpr/ppermute | solution.py:16
  125.5 13.6 %collective-permute-start = (bf16[2,256,512]{2,1,0:T(8,128)(2,1)}, bf16[2,256,512]{2,1,0:T(8,128)(2,1)S(1)}, u32[]{:S(2)}, u32[]{:S(2)}) collective-permute-start(bf16[2,256,512]{2,1,0:T(8,128)(2,1)} %get-tuple-element.288), channel_id=1, source_target_pairs={{124,0},{0,4},{4,8},{8,12},{12,16},{16,20},{20,24},{24,28},{28,32}... | collective-permute-start | bytes 1572872 | tf_op jit(solution)/shard_map/while/body/eval_jaxpr/ppermute | solution.py:16
  140.7 13.7 %collective-permute-start = (bf16[2,256,512]{2,1,0:T(8,128)(2,1)}, bf16[2,256,512]{2,1,0:T(8,128)(2,1)S(1)}, u32[]{:S(2)}, u32[]{:S(2)}) collective-permute-start(bf16[2,256,512]{2,1,0:T(8,128)(2,1)} %get-tuple-element.288), channel_id=1, source_target_pairs={{124,0},{0,4},{4,8},{8,12},{12,16},{16,20},{20,24},{24,28},{28,32}... | collective-permute-start | bytes 1572872 | tf_op jit(solution)/shard_map/while/body/eval_jaxpr/ppermute | solution.py:16
  156.1 14.8 %collective-permute-start = (bf16[2,256,512]{2,1,0:T(8,128)(2,1)}, bf16[2,256,512]{2,1,0:T(8,128)(2,1)S(1)}, u32[]{:S(2)}, u32[]{:S(2)}) collective-permute-start(bf16[2,256,512]{2,1,0:T(8,128)(2,1)} %get-tuple-element.288), channel_id=1, source_target_pairs={{124,0},{0,4},{4,8},{8,12},{12,16},{16,20},{20,24},{24,28},{28,32}... | collective-permute-start | bytes 1572872 | tf_op jit(solution)/shard_map/while/body/eval_jaxpr/ppermute | solution.py:16
  172.5 15.9 %collective-permute-start = (bf16[2,256,512]{2,1,0:T(8,128)(2,1)}, bf16[2,256,512]{2,1,0:T(8,128)(2,1)S(1)}, u32[]{:S(2)}, u32[]{:S(2)}) collective-permute-start(bf16[2,256,512]{2,1,0:T(8,128)(2,1)} %get-tuple-element.288), channel_id=1, source_target_pairs={{124,0},{0,4},{4,8},{8,12},{12,16},{16,20},{20,24},{24,28},{28,32}... | collective-permute-start | bytes 1572872 | tf_op jit(solution)/shard_map/while/body/eval_jaxpr/ppermute | solution.py:16
  190.0 17.0 %collective-permute-start = (bf16[2,256,512]{2,1,0:T(8,128)(2,1)}, bf16[2,256,512]{2,1,0:T(8,128)(2,1)S(1)}, u32[]{:S(2)}, u32[]{:S(2)}) collective-permute-start(bf16[2,256,512]{2,1,0:T(8,128)(2,1)} %get-tuple-element.288), channel_id=1, source_target_pairs={{124,0},{0,4},{4,8},{8,12},{12,16},{16,20},{20,24},{24,28},{28,32}... | collective-permute-start | bytes 1572872 | tf_op jit(solution)/shard_map/while/body/eval_jaxpr/ppermute | solution.py:16
  208.6 18.1 %collective-permute-start = (bf16[2,256,512]{2,1,0:T(8,128)(2,1)}, bf16[2,256,512]{2,1,0:T(8,128)(2,1)S(1)}, u32[]{:S(2)}, u32[]{:S(2)}) collective-permute-start(bf16[2,256,512]{2,1,0:T(8,128)(2,1)} %get-tuple-element.288), channel_id=1, source_target_pairs={{124,0},{0,4},{4,8},{8,12},{12,16},{16,20},{20,24},{24,28},{28,32}... | collective-permute-start | bytes 1572872 | tf_op jit(solution)/shard_map/while/body/eval_jaxpr/ppermute | solution.py:16
  228.3 19.2 %collective-permute-start = (bf16[2,256,512]{2,1,0:T(8,128)(2,1)}, bf16[2,256,512]{2,1,0:T(8,128)(2,1)S(1)}, u32[]{:S(2)}, u32[]{:S(2)}) collective-permute-start(bf16[2,256,512]{2,1,0:T(8,128)(2,1)} %get-tuple-element.288), channel_id=1, source_target_pairs={{124,0},{0,4},{4,8},{8,12},{12,16},{16,20},{20,24},{24,28},{28,32}... | collective-permute-start | bytes 1572872 | tf_op jit(solution)/shard_map/while/body/eval_jaxpr/ppermute | solution.py:16
  249.1 18.4 %collective-permute-start = (bf16[2,256,512]{2,1,0:T(8,128)(2,1)}, bf16[2,256,512]{2,1,0:T(8,128)(2,1)S(1)}, u32[]{:S(2)}, u32[]{:S(2)}) collective-permute-start(bf16[2,256,512]{2,1,0:T(8,128)(2,1)} %get-tuple-element.288), channel_id=1, source_target_pairs={{124,0},{0,4},{4,8},{8,12},{12,16},{16,20},{20,24},{24,28},{28,32}... | collective-permute-start | bytes 1572872 | tf_op jit(solution)/shard_map/while/body/eval_jaxpr/ppermute | solution.py:16
  269.1 17.5 %collective-permute-start = (bf16[2,256,512]{2,1,0:T(8,128)(2,1)}, bf16[2,256,512]{2,1,0:T(8,128)(2,1)S(1)}, u32[]{:S(2)}, u32[]{:S(2)}) collective-permute-start(bf16[2,256,512]{2,1,0:T(8,128)(2,1)} %get-tuple-element.288), channel_id=1, source_target_pairs={{124,0},{0,4},{4,8},{8,12},{12,16},{16,20},{20,24},{24,28},{28,32}... | collective-permute-start | bytes 1572872 | tf_op jit(solution)/shard_map/while/body/eval_jaxpr/ppermute | solution.py:16
  288.3 13.6 %collective-permute-start = (bf16[2,256,512]{2,1,0:T(8,128)(2,1)}, bf16[2,256,512]{2,1,0:T(8,128)(2,1)S(1)}, u32[]{:S(2)}, u32[]{:S(2)}) collective-permute-start(bf16[2,256,512]{2,1,0:T(8,128)(2,1)} %get-tuple-element.288), channel_id=1, source_target_pairs={{124,0},{0,4},{4,8},{8,12},{12,16},{16,20},{20,24},{24,28},{28,32}... | collective-permute-start | bytes 1572872 | tf_op jit(solution)/shard_map/while/body/eval_jaxpr/ppermute | solution.py:16
  356.3 4.9 copy-start.13
  366.0 9.2 slice-start.6
  366.0 9.2 slice-start.12
  366.0 9.2 slice-start.7
  366.0 9.2 slice-start.13
  390.2 4.9 copy-start.12
  399.9 9.2 slice-start.8
  399.9 9.2 slice-start.14
  399.9 9.2 slice-start.9
  399.9 9.2 slice-start.15
  403.6 4.1 copy-start.8
  424.4 4.9 copy-start.11
  434.0 9.2 slice-start.10
  434.0 9.2 slice-start.16
  434.0 9.2 slice-start.11
  434.0 9.2 slice-start.17
  437.7 4.1 copy-start.9
  437.7 4.1 copy-start.15
  487.3 5.4 copy-start.10
  496.6 8.4 copy-start.14
  501.4 7.4 slice-start.4
  501.4 7.4 slice-start.18
  501.4 7.4 slice-start.5
  501.4 7.8 slice-start.19
  588.4 8.0 copy-start.27
  607.1 5.9 slice-start
  665.9 24.6 %collective-permute-start.1 = (f32[2,256,512]{2,1,0:T(8,128)S(1)}, f32[2,256,512]{2,1,0:T(8,128)S(1)}, u32[]{:S(2)}, u32[]{:S(2)}) collective-permute-start(f32[2,256,512]{2,1,0:T(8,128)S(1)} %get-tuple-element.308), channel_id=1, source_target_pairs={{4,0},{8,4},{12,8},{16,12},{20,16},{24,20},{28,24},{32,28},{36,32}... | collective-permute-start | bytes 3145736 | tf_op jit(solution)/shard_map/while/body/eval_jaxpr/ppermute | solution.py:16
  691.9 28.1 %collective-permute-start.1 = (f32[2,256,512]{2,1,0:T(8,128)S(1)}, f32[2,256,512]{2,1,0:T(8,128)S(1)}, u32[]{:S(2)}, u32[]{:S(2)}) collective-permute-start(f32[2,256,512]{2,1,0:T(8,128)S(1)} %get-tuple-element.308), channel_id=1, source_target_pairs={{4,0},{8,4},{12,8},{16,12},{20,16},{24,20},{28,24},{32,28},{36,32}... | collective-permute-start | bytes 3145736 | tf_op jit(solution)/shard_map/while/body/eval_jaxpr/ppermute | solution.py:16
  721.4 27.9 %collective-permute-start.1 = (f32[2,256,512]{2,1,0:T(8,128)S(1)}, f32[2,256,512]{2,1,0:T(8,128)S(1)}, u32[]{:S(2)}, u32[]{:S(2)}) collective-permute-start(f32[2,256,512]{2,1,0:T(8,128)S(1)} %get-tuple-element.308), channel_id=1, source_target_pairs={{4,0},{8,4},{12,8},{16,12},{20,16},{24,20},{28,24},{32,28},{36,32}... | collective-permute-start | bytes 3145736 | tf_op jit(solution)/shard_map/while/body/eval_jaxpr/ppermute | solution.py:16
  750.8 27.0 %collective-permute-start.1 = (f32[2,256,512]{2,1,0:T(8,128)S(1)}, f32[2,256,512]{2,1,0:T(8,128)S(1)}, u32[]{:S(2)}, u32[]{:S(2)}) collective-permute-start(f32[2,256,512]{2,1,0:T(8,128)S(1)} %get-tuple-element.308), channel_id=1, source_target_pairs={{4,0},{8,4},{12,8},{16,12},{20,16},{24,20},{28,24},{32,28},{36,32}... | collective-permute-start | bytes 3145736 | tf_op jit(solution)/shard_map/while/body/eval_jaxpr/ppermute | solution.py:16
  779.2 26.1 %collective-permute-start.1 = (f32[2,256,512]{2,1,0:T(8,128)S(1)}, f32[2,256,512]{2,1,0:T(8,128)S(1)}, u32[]{:S(2)}, u32[]{:S(2)}) collective-permute-start(f32[2,256,512]{2,1,0:T(8,128)S(1)} %get-tuple-element.308), channel_id=1, source_target_pairs={{4,0},{8,4},{12,8},{16,12},{20,16},{24,20},{28,24},{32,28},{36,32}... | collective-permute-start | bytes 3145736 | tf_op jit(solution)/shard_map/while/body/eval_jaxpr/ppermute | solution.py:16
  806.7 25.2 %collective-permute-start.1 = (f32[2,256,512]{2,1,0:T(8,128)S(1)}, f32[2,256,512]{2,1,0:T(8,128)S(1)}, u32[]{:S(2)}, u32[]{:S(2)}) collective-permute-start(f32[2,256,512]{2,1,0:T(8,128)S(1)} %get-tuple-element.308), channel_id=1, source_target_pairs={{4,0},{8,4},{12,8},{16,12},{20,16},{24,20},{28,24},{32,28},{36,32}... | collective-permute-start | bytes 3145736 | tf_op jit(solution)/shard_map/while/body/eval_jaxpr/ppermute | solution.py:16
  833.3 24.2 %collective-permute-start.1 = (f32[2,256,512]{2,1,0:T(8,128)S(1)}, f32[2,256,512]{2,1,0:T(8,128)S(1)}, u32[]{:S(2)}, u32[]{:S(2)}) collective-permute-start(f32[2,256,512]{2,1,0:T(8,128)S(1)} %get-tuple-element.308), channel_id=1, source_target_pairs={{4,0},{8,4},{12,8},{16,12},{20,16},{24,20},{28,24},{32,28},{36,32}... | collective-permute-start | bytes 3145736 | tf_op jit(solution)/shard_map/while/body/eval_jaxpr/ppermute | solution.py:16
  859.0 23.3 %collective-permute-start.1 = (f32[2,256,512]{2,1,0:T(8,128)S(1)}, f32[2,256,512]{2,1,0:T(8,128)S(1)}, u32[]{:S(2)}, u32[]{:S(2)}) collective-permute-start(f32[2,256,512]{2,1,0:T(8,128)S(1)} %get-tuple-element.308), channel_id=1, source_target_pairs={{4,0},{8,4},{12,8},{16,12},{20,16},{24,20},{28,24},{32,28},{36,32}... | collective-permute-start | bytes 3145736 | tf_op jit(solution)/shard_map/while/body/eval_jaxpr/ppermute | solution.py:16
  883.8 22.4 %collective-permute-start.1 = (f32[2,256,512]{2,1,0:T(8,128)S(1)}, f32[2,256,512]{2,1,0:T(8,128)S(1)}, u32[]{:S(2)}, u32[]{:S(2)}) collective-permute-start(f32[2,256,512]{2,1,0:T(8,128)S(1)} %get-tuple-element.308), channel_id=1, source_target_pairs={{4,0},{8,4},{12,8},{16,12},{20,16},{24,20},{28,24},{32,28},{36,32}... | collective-permute-start | bytes 3145736 | tf_op jit(solution)/shard_map/while/body/eval_jaxpr/ppermute | solution.py:16
  907.6 21.9 %collective-permute-start.1 = (f32[2,256,512]{2,1,0:T(8,128)S(1)}, f32[2,256,512]{2,1,0:T(8,128)S(1)}, u32[]{:S(2)}, u32[]{:S(2)}) collective-permute-start(f32[2,256,512]{2,1,0:T(8,128)S(1)} %get-tuple-element.308), channel_id=1, source_target_pairs={{4,0},{8,4},{12,8},{16,12},{20,16},{24,20},{28,24},{32,28},{36,32}... | collective-permute-start | bytes 3145736 | tf_op jit(solution)/shard_map/while/body/eval_jaxpr/ppermute | solution.py:16
  930.9 21.9 %collective-permute-start.1 = (f32[2,256,512]{2,1,0:T(8,128)S(1)}, f32[2,256,512]{2,1,0:T(8,128)S(1)}, u32[]{:S(2)}, u32[]{:S(2)}) collective-permute-start(f32[2,256,512]{2,1,0:T(8,128)S(1)} %get-tuple-element.308), channel_id=1, source_target_pairs={{4,0},{8,4},{12,8},{16,12},{20,16},{24,20},{28,24},{32,28},{36,32}... | collective-permute-start | bytes 3145736 | tf_op jit(solution)/shard_map/while/body/eval_jaxpr/ppermute | solution.py:16
  954.3 21.9 %collective-permute-start.1 = (f32[2,256,512]{2,1,0:T(8,128)S(1)}, f32[2,256,512]{2,1,0:T(8,128)S(1)}, u32[]{:S(2)}, u32[]{:S(2)}) collective-permute-start(f32[2,256,512]{2,1,0:T(8,128)S(1)} %get-tuple-element.308), channel_id=1, source_target_pairs={{4,0},{8,4},{12,8},{16,12},{20,16},{24,20},{28,24},{32,28},{36,32}... | collective-permute-start | bytes 3145736 | tf_op jit(solution)/shard_map/while/body/eval_jaxpr/ppermute | solution.py:16
  977.6 22.3 %collective-permute-start.1 = (f32[2,256,512]{2,1,0:T(8,128)S(1)}, f32[2,256,512]{2,1,0:T(8,128)S(1)}, u32[]{:S(2)}, u32[]{:S(2)}) collective-permute-start(f32[2,256,512]{2,1,0:T(8,128)S(1)} %get-tuple-element.308), channel_id=1, source_target_pairs={{4,0},{8,4},{12,8},{16,12},{20,16},{24,20},{28,24},{32,28},{36,32}... | collective-permute-start | bytes 3145736 | tf_op jit(solution)/shard_map/while/body/eval_jaxpr/ppermute | solution.py:16
  1001.3 23.4 %collective-permute-start.1 = (f32[2,256,512]{2,1,0:T(8,128)S(1)}, f32[2,256,512]{2,1,0:T(8,128)S(1)}, u32[]{:S(2)}, u32[]{:S(2)}) collective-permute-start(f32[2,256,512]{2,1,0:T(8,128)S(1)} %get-tuple-element.308), channel_id=1, source_target_pairs={{4,0},{8,4},{12,8},{16,12},{20,16},{24,20},{28,24},{32,28},{36,32}... | collective-permute-start | bytes 3145736 | tf_op jit(solution)/shard_map/while/body/eval_jaxpr/ppermute | solution.py:16
  1026.1 24.5 %collective-permute-start.1 = (f32[2,256,512]{2,1,0:T(8,128)S(1)}, f32[2,256,512]{2,1,0:T(8,128)S(1)}, u32[]{:S(2)}, u32[]{:S(2)}) collective-permute-start(f32[2,256,512]{2,1,0:T(8,128)S(1)} %get-tuple-element.308), channel_id=1, source_target_pairs={{4,0},{8,4},{12,8},{16,12},{20,16},{24,20},{28,24},{32,28},{36,32}... | collective-permute-start | bytes 3145736 | tf_op jit(solution)/shard_map/while/body/eval_jaxpr/ppermute | solution.py:16
  1052.0 19.1 %collective-permute-start.1 = (f32[2,256,512]{2,1,0:T(8,128)S(1)}, f32[2,256,512]{2,1,0:T(8,128)S(1)}, u32[]{:S(2)}, u32[]{:S(2)}) collective-permute-start(f32[2,256,512]{2,1,0:T(8,128)S(1)} %get-tuple-element.308), channel_id=1, source_target_pairs={{4,0},{8,4},{12,8},{16,12},{20,16},{24,20},{28,24},{32,28},{36,32}... | collective-permute-start | bytes 3145736 | tf_op jit(solution)/shard_map/while/body/eval_jaxpr/ppermute | solution.py:16
  1072.6 4.9 copy-start.19
  1072.6 4.9 copy-start.20
  1072.6 4.9 copy-start.21
  1073.4 10.9 %collective-permute-start.3 = (bf16[2,256,512]{2,1,0:T(8,128)(2,1)}, bf16[2,256,512]{2,1,0:T(8,128)(2,1)}, u32[]{:S(2)}, u32[]{:S(2)}) collective-permute-start(bf16[2,256,512]{2,1,0:T(8,128)(2,1)} %convert_element_type.84), channel_id=1, source_target_pairs={{96,0},{100,4},{104,8},{108,12},{112,16},{116,20},{120,24},{124,28... | collective-permute-start | bytes 1572872 | tf_op jit(solution)/shard_map/ppermute | solution.py:16
  (20 other events, 55.0 us)
where the time goes:
time: 1100 us; the launch traced here: 1090 us
  waiting for transfers between devices  536 us (49%)
  local copies, waits for them, and re-layouts  211 us (19%)
  matrix products  114 us (10%)
  starting transfers between devices  107 us (10%)
  blocking collectives  63.8 us (6%)
  other arithmetic  52.3 us (5%)
    ppermute x34, waiting for transfers between devices, passed_along(): return lax.ppermute(block, axis, route)  536 us
    ppermute x34, starting transfers between devices, passed_along(): return lax.ppermute(block, axis, route)  107 us
    psum x1, blocking collectives, body(): scale_total = lax.psum(jnp.stack(scale_parts), ('ctx', 'batch'))  63.8 us
    another operation x6, local copies, waits for them, and re-layouts, body(): jnp.stack(placed_parts)  24.6 us
    dot_general x4, matrix products, body(): jnp.einsum('sw,csx->cwx', chooser, both_parts, precision=lax.Precision.HI...  24.4 us
    slice x1, local copies, waits for them, and re-layouts, body(): blocks_all[0, :, :, group_id]  23.1 us
    add x16, other arithmetic, chain_turn(): moved + lax.dynamic_index_in_dim(grads_window, turn_no, 0, keepdims=False)  22.9 us
  transfers between devices with their start and end apart: 34, of which 34 were waited for; matrix products, arithmetic and copies ran while one was open for 2% of the time, Pallas kernels for 0%

commit v1 on v0

--- a/solution.py
+++ b/solution.py
@@ -113,7 +113,7 @@
     )
     key_grad = summed[0].reshape(1, tokens, KV_HEADS * HD).astype(jnp.bfloat16)
     value_grad = summed[1].reshape(1, tokens, KV_HEADS * HD).astype(jnp.bfloat16)
-    scale_total = lax.psum(jnp.stack(scale_parts), ("ctx", "batch"))
+    scale_total = lax.psum(lax.psum(jnp.stack(scale_parts), "ctx"), "batch")
     tau_grad = scale_total.reshape(HEADS) / math.sqrt(lax.axis_size("batch") * ctx_size * tokens)
     return (attended, query_grad, key_grad, value_grad, tau_grad)
 

time: 1100 us -> 1110 us (level)
  blocking collectives: 63.8 us -> 84.2 us
    psum x1 -> x2, blocking collectives: 63.8 us -> 84.2 us  [body(): scale_total = lax.psum(lax.psum(jnp.stack(scale_parts), 'ctx'), 'batch')]
where the time goes in v1:
time: 1110 us
  waiting for transfers between devices  534 us (48%)
  local copies, waits for them, and re-layouts  212 us (19%)
  matrix products  115 us (10%)
  starting transfers between devices  108 us (10%)
  blocking collectives  84.2 us (8%)
  other arithmetic  50.9 us (5%)
    ppermute x34, waiting for transfers between devices, passed_along(): return lax.ppermute(block, axis, route)  534 us
    ppermute x34, starting transfers between devices, passed_along(): return lax.ppermute(block, axis, route)  108 us
    psum x2, blocking collectives, body(): scale_total = lax.psum(lax.psum(jnp.stack(scale_parts), 'ctx'), 'batch')  84.2 us
    dot_general x4, matrix products, body(): jnp.einsum('sw,csx->cwx', chooser, both_parts, precision=lax.Precision.HI...  25.9 us
    another operation x6, local copies, waits for them, and re-layouts, body(): jnp.stack(placed_parts)  24.5 us
    slice x1, local copies, waits for them, and re-layouts, body(): blocks_all[0, :, :, group_id]  23.5 us
    add x16, other arithmetic, chain_turn(): moved + lax.dynamic_index_in_dim(grads_window, turn_no, 0, keepdims=False)  22.9 us
  transfers between devices with their start and end apart: 34, of which 34 were waited for; matrix products, arithmetic and copies ran while one was open for 2% of the time, Pallas kernels for 0%

profile of v1, /device:TPU:0, one launch (start us, length us, event | category | flops | bytes accessed | tf_op | source)
XLA Modules:
  0.0 1105.4 jit_solution(8288937326459912877)
XLA Ops:
  17.2 5.5 dynamic_update_slice.10
  22.7 281.0 %while.30 = (s32[]{:T(128)}, bf16[2,256,512]{2,1,0:T(8,128)(2,1)}, bf16[2,17,256,512]{3,2,0,1:T(8,128)(2,1)}, s32[]{:T(128)}, s32[]{:T(128)}, /*index=5*/s32[]{:T(128)}, s32[]{:T(128)}) while((s32[]{:T(128)}, bf16[2,256,512]{2,1,0:T(8,128)(2,1)}, bf16[2,17,256,512]{3,2,0,1:T(8,128)(2,1)}, s32[]{:T(128)}, s32[]{:T(128)}, /*index=5*/s32[]{:T(128)}, ...), condition=%wide.region_1.0_spmd, body=%wide.region_0.0_spmd.sunk | while | flops 6 | bytes 4194471 | solution.py:43
  24.6 16.6 %collective-permute-done = bf16[2,256,512]{2,1,0:T(8,128)(2,1)S(1)} collective-permute-done((bf16[2,256,512]{2,1,0:T(8,128)(2,1)}, bf16[2,256,512]{2,1,0:T(8,128)(2,1)S(1)}, u32[]{:S(2)}, u32[]{:S(2)}) %collective-permute-start) | collective-permute-done | bytes 524320 | tf_op jit(solution)/shard_map/while/body/eval_jaxpr/ppermute | solution.py:16
  42.9 16.6 %collective-permute-done = bf16[2,256,512]{2,1,0:T(8,128)(2,1)S(1)} collective-permute-done((bf16[2,256,512]{2,1,0:T(8,128)(2,1)}, bf16[2,256,512]{2,1,0:T(8,128)(2,1)S(1)}, u32[]{:S(2)}, u32[]{:S(2)}) %collective-permute-start) | collective-permute-done | bytes 524320 | tf_op jit(solution)/shard_map/while/body/eval_jaxpr/ppermute | solution.py:16
  61.2 15.7 %collective-permute-done = bf16[2,256,512]{2,1,0:T(8,128)(2,1)S(1)} collective-permute-done((bf16[2,256,512]{2,1,0:T(8,128)(2,1)}, bf16[2,256,512]{2,1,0:T(8,128)(2,1)S(1)}, u32[]{:S(2)}, u32[]{:S(2)}) %collective-permute-start) | collective-permute-done | bytes 524320 | tf_op jit(solution)/shard_map/while/body/eval_jaxpr/ppermute | solution.py:16
  78.5 14.7 %collective-permute-done = bf16[2,256,512]{2,1,0:T(8,128)(2,1)S(1)} collective-permute-done((bf16[2,256,512]{2,1,0:T(8,128)(2,1)}, bf16[2,256,512]{2,1,0:T(8,128)(2,1)S(1)}, u32[]{:S(2)}, u32[]{:S(2)}) %collective-permute-start) | collective-permute-done | bytes 524320 | tf_op jit(solution)/shard_map/while/body/eval_jaxpr/ppermute | solution.py:16
  94.8 13.8 %collective-permute-done = bf16[2,256,512]{2,1,0:T(8,128)(2,1)S(1)} collective-permute-done((bf16[2,256,512]{2,1,0:T(8,128)(2,1)}, bf16[2,256,512]{2,1,0:T(8,128)(2,1)S(1)}, u32[]{:S(2)}, u32[]{:S(2)}) %collective-permute-start) | collective-permute-done | bytes 524320 | tf_op jit(solution)/shard_map/while/body/eval_jaxpr/ppermute | solution.py:16
  110.3 13.6 %collective-permute-done = bf16[2,256,512]{2,1,0:T(8,128)(2,1)S(1)} collective-permute-done((bf16[2,256,512]{2,1,0:T(8,128)(2,1)}, bf16[2,256,512]{2,1,0:T(8,128)(2,1)S(1)}, u32[]{:S(2)}, u32[]{:S(2)}) %collective-permute-start) | collective-permute-done | bytes 524320 | tf_op jit(solution)/shard_map/while/body/eval_jaxpr/ppermute | solution.py:16
  125.6 13.6 %collective-permute-done = bf16[2,256,512]{2,1,0:T(8,128)(2,1)S(1)} collective-permute-done((bf16[2,256,512]{2,1,0:T(8,128)(2,1)}, bf16[2,256,512]{2,1,0:T(8,128)(2,1)S(1)}, u32[]{:S(2)}, u32[]{:S(2)}) %collective-permute-start) | collective-permute-done | bytes 524320 | tf_op jit(solution)/shard_map/while/body/eval_jaxpr/ppermute | solution.py:16
  140.9 13.7 %collective-permute-done = bf16[2,256,512]{2,1,0:T(8,128)(2,1)S(1)} collective-permute-done((bf16[2,256,512]{2,1,0:T(8,128)(2,1)}, bf16[2,256,512]{2,1,0:T(8,128)(2,1)S(1)}, u32[]{:S(2)}, u32[]{:S(2)}) %collective-permute-start) | collective-permute-done | bytes 524320 | tf_op jit(solution)/shard_map/while/body/eval_jaxpr/ppermute | solution.py:16
  156.2 14.8 %collective-permute-done = bf16[2,256,512]{2,1,0:T(8,128)(2,1)S(1)} collective-permute-done((bf16[2,256,512]{2,1,0:T(8,128)(2,1)}, bf16[2,256,512]{2,1,0:T(8,128)(2,1)S(1)}, u32[]{:S(2)}, u32[]{:S(2)}) %collective-permute-start) | collective-permute-done | bytes 524320 | tf_op jit(solution)/shard_map/while/body/eval_jaxpr/ppermute | solution.py:16
  172.6 15.8 %collective-permute-done = bf16[2,256,512]{2,1,0:T(8,128)(2,1)S(1)} collective-permute-done((bf16[2,256,512]{2,1,0:T(8,128)(2,1)}, bf16[2,256,512]{2,1,0:T(8,128)(2,1)S(1)}, u32[]{:S(2)}, u32[]{:S(2)}) %collective-permute-start) | collective-permute-done | bytes 524320 | tf_op jit(solution)/shard_map/while/body/eval_jaxpr/ppermute | solution.py:16
  190.1 16.9 %collective-permute-done = bf16[2,256,512]{2,1,0:T(8,128)(2,1)S(1)} collective-permute-done((bf16[2,256,512]{2,1,0:T(8,128)(2,1)}, bf16[2,256,512]{2,1,0:T(8,128)(2,1)S(1)}, u32[]{:S(2)}, u32[]{:S(2)}) %collective-permute-start) | collective-permute-done | bytes 524320 | tf_op jit(solution)/shard_map/while/body/eval_jaxpr/ppermute | solution.py:16
  208.7 18.1 %collective-permute-done = bf16[2,256,512]{2,1,0:T(8,128)(2,1)S(1)} collective-permute-done((bf16[2,256,512]{2,1,0:T(8,128)(2,1)}, bf16[2,256,512]{2,1,0:T(8,128)(2,1)S(1)}, u32[]{:S(2)}, u32[]{:S(2)}) %collective-permute-start) | collective-permute-done | bytes 524320 | tf_op jit(solution)/shard_map/while/body/eval_jaxpr/ppermute | solution.py:16
  228.4 19.2 %collective-permute-done = bf16[2,256,512]{2,1,0:T(8,128)(2,1)S(1)} collective-permute-done((bf16[2,256,512]{2,1,0:T(8,128)(2,1)}, bf16[2,256,512]{2,1,0:T(8,128)(2,1)S(1)}, u32[]{:S(2)}, u32[]{:S(2)}) %collective-permute-start) | collective-permute-done | bytes 524320 | tf_op jit(solution)/shard_map/while/body/eval_jaxpr/ppermute | solution.py:16
  249.3 18.4 %collective-permute-done = bf16[2,256,512]{2,1,0:T(8,128)(2,1)S(1)} collective-permute-done((bf16[2,256,512]{2,1,0:T(8,128)(2,1)}, bf16[2,256,512]{2,1,0:T(8,128)(2,1)S(1)}, u32[]{:S(2)}, u32[]{:S(2)}) %collective-permute-start) | collective-permute-done | bytes 524320 | tf_op jit(solution)/shard_map/while/body/eval_jaxpr/ppermute | solution.py:16
  269.3 17.5 %collective-permute-done = bf16[2,256,512]{2,1,0:T(8,128)(2,1)S(1)} collective-permute-done((bf16[2,256,512]{2,1,0:T(8,128)(2,1)}, bf16[2,256,512]{2,1,0:T(8,128)(2,1)S(1)}, u32[]{:S(2)}, u32[]{:S(2)}) %collective-permute-start) | collective-permute-done | bytes 524320 | tf_op jit(solution)/shard_map/while/body/eval_jaxpr/ppermute | solution.py:16
  288.5 13.6 %collective-permute-done = bf16[2,256,512]{2,1,0:T(8,128)(2,1)S(1)} collective-permute-done((bf16[2,256,512]{2,1,0:T(8,128)(2,1)}, bf16[2,256,512]{2,1,0:T(8,128)(2,1)S(1)}, u32[]{:S(2)}, u32[]{:S(2)}) %collective-permute-start) | collective-permute-done | bytes 524320 | tf_op jit(solution)/shard_map/while/body/eval_jaxpr/ppermute | solution.py:16
  303.8 8.0 copy.85
  311.8 13.4 %reshape.174 = bf16[2,34,128,4,128]{4,3,2,1,0:T(4,128)(2,1)} reshape(bf16[2,17,256,512]{3,2,1,0:T(8,128)(2,1)} %copy.85) | data formatting | bytes 17825792 | tf_op jit(solution)/shard_map/reshape | solution.py:44
  325.1 23.5 %fusion.82 = (bf16[1,34,128,1,128]{4,3,2,1,0:T(2,128)(2,1)S(1)}, bf16[1,34,128,1,128]{4,3,2,1,0:T(2,128)(2,1)}, bf16[1,34,128,1,128]{4,3,2,1,0:T(2,128)(2,1)}, b...) fusion(bf16[2,34,128,4,128]{4,3,2,1,0:T(4,128)(2,1)} %reshape.174), kind=kLoop, calls=%fused_computation.196 | loop fusion | bytes 17825792 | tf_op jit(solution)/shard_map/slice | solution.py:59
  357.0 4.9 fusion.57
  460.3 6.5 convolution_bitcast_fusion.2
  475.4 6.5 convolution_bitcast_fusion.1
  490.6 6.5 convolution_bitcast_fusion
  523.0 76.8 %psum.14 = f32[4,4]{1,0:T(4,128)S(1)} all-reduce(f32[4,4]{1,0:T(4,128)S(1)} %pad_maximum_fusion.3), channel_id=1, replica_groups=mesh['ctx'=32,'batch'=4] {'ctx'}, use_global_device_ids=true, to_apply=%region_20.22 | all-reduce | flops 16 | bytes 128 | tf_op jit(solution)/shard_map/psum | solution.py:116
  599.8 7.4 psum.15
  609.4 5.2 convolution_bitcast_fusion.11
  617.4 6.5 convolution_bitcast_fusion.3
  635.8 6.7 copy.256
  642.4 19.9 %copy.128 = f32[17,2,2,128,4,128]{5,4,3,2,1,0:T(4,128)} copy(f32[17,2,2,128,4,128]{5,3,2,0,1,4:T(8,128)S(1)} %bitcast.371) | data formatting | bytes 35651584 | tf_op jit(solution)/shard_map/transpose | solution.py:104
  662.3 21.9 %reshape.183 = f32[17,2,256,512]{3,2,1,0:T(8,128)} reshape(f32[17,2,2,128,4,128]{5,4,3,2,1,0:T(4,128)} %copy.128) | data formatting | bytes 35651584 | tf_op jit(solution)/shard_map/reshape | solution.py:104
  686.7 404.6 %while.31 = (s32[]{:T(128)}, f32[2,256,512]{2,1,0:T(8,128)S(1)}, f32[17,2,256,512]{3,2,1,0:T(8,128)}, s32[]{:T(128)}, s32[]{:T(128)}, /*index=5*/s32[]{:T(128)}) while((s32[]{:T(128)}, f32[2,256,512]{2,1,0:T(8,128)S(1)}, f32[17,2,256,512]{3,2,1,0:T(8,128)}, s32[]{:T(128)}, s32[]{:T(128)}, /*index=5*/s32[]{:T(128)}) %tuple.109), condition=%wide.region_15.17_spmd, body=%wide.region_14.16_spmd.sunk | while | flops 262149 | bytes 7340179 | solution.py:110
  688.7 23.4 %collective-permute-done.1 = f32[2,256,512]{2,1,0:T(8,128)S(1)} collective-permute-done((f32[2,256,512]{2,1,0:T(8,128)S(1)}, f32[2,256,512]{2,1,0:T(8,128)S(1)}, u32[]{:S(2)}, u32[]{:S(2)}) %collective-permute-start.1) | collective-permute-done | bytes 1048608 | tf_op jit(solution)/shard_map/while/body/eval_jaxpr/ppermute | solution.py:16
  713.5 5.8 collective-permute-start.1
  719.4 21.6 %collective-permute-done.1 = f32[2,256,512]{2,1,0:T(8,128)S(1)} collective-permute-done((f32[2,256,512]{2,1,0:T(8,128)S(1)}, f32[2,256,512]{2,1,0:T(8,128)S(1)}, u32[]{:S(2)}, u32[]{:S(2)}) %collective-permute-start.1) | collective-permute-done | bytes 1048608 | tf_op jit(solution)/shard_map/while/body/eval_jaxpr/ppermute | solution.py:16
  742.4 6.8 collective-permute-start.1
  749.1 20.6 %collective-permute-done.1 = f32[2,256,512]{2,1,0:T(8,128)S(1)} collective-permute-done((f32[2,256,512]{2,1,0:T(8,128)S(1)}, f32[2,256,512]{2,1,0:T(8,128)S(1)}, u32[]{:S(2)}, u32[]{:S(2)}) %collective-permute-start.1) | collective-permute-done | bytes 1048608 | tf_op jit(solution)/shard_map/while/body/eval_jaxpr/ppermute | solution.py:16
  771.2 6.8 collective-permute-start.1
  778.0 19.7 %collective-permute-done.1 = f32[2,256,512]{2,1,0:T(8,128)S(1)} collective-permute-done((f32[2,256,512]{2,1,0:T(8,128)S(1)}, f32[2,256,512]{2,1,0:T(8,128)S(1)}, u32[]{:S(2)}, u32[]{:S(2)}) %collective-permute-start.1) | collective-permute-done | bytes 1048608 | tf_op jit(solution)/shard_map/while/body/eval_jaxpr/ppermute | solution.py:16
  799.1 6.8 collective-permute-start.1
  805.9 18.8 %collective-permute-done.1 = f32[2,256,512]{2,1,0:T(8,128)S(1)} collective-permute-done((f32[2,256,512]{2,1,0:T(8,128)S(1)}, f32[2,256,512]{2,1,0:T(8,128)S(1)}, u32[]{:S(2)}, u32[]{:S(2)}) %collective-permute-start.1) | collective-permute-done | bytes 1048608 | tf_op jit(solution)/shard_map/while/body/eval_jaxpr/ppermute | solution.py:16
  826.1 6.8 collective-permute-start.1
  832.9 17.9 %collective-permute-done.1 = f32[2,256,512]{2,1,0:T(8,128)S(1)} collective-permute-done((f32[2,256,512]{2,1,0:T(8,128)S(1)}, f32[2,256,512]{2,1,0:T(8,128)S(1)}, u32[]{:S(2)}, u32[]{:S(2)}) %collective-permute-start.1) | collective-permute-done | bytes 1048608 | tf_op jit(solution)/shard_map/while/body/eval_jaxpr/ppermute | solution.py:16
  852.2 6.8 collective-permute-start.1
  859.0 16.9 %collective-permute-done.1 = f32[2,256,512]{2,1,0:T(8,128)S(1)} collective-permute-done((f32[2,256,512]{2,1,0:T(8,128)S(1)}, f32[2,256,512]{2,1,0:T(8,128)S(1)}, u32[]{:S(2)}, u32[]{:S(2)}) %collective-permute-start.1) | collective-permute-done | bytes 1048608 | tf_op jit(solution)/shard_map/while/body/eval_jaxpr/ppermute | solution.py:16
  877.4 6.8 collective-permute-start.1
  884.2 16.0 %collective-permute-done.1 = f32[2,256,512]{2,1,0:T(8,128)S(1)} collective-permute-done((f32[2,256,512]{2,1,0:T(8,128)S(1)}, f32[2,256,512]{2,1,0:T(8,128)S(1)}, u32[]{:S(2)}, u32[]{:S(2)}) %collective-permute-start.1) | collective-permute-done | bytes 1048608 | tf_op jit(solution)/shard_map/while/body/eval_jaxpr/ppermute | solution.py:16
  901.6 6.8 collective-permute-start.1
  908.4 15.1 %collective-permute-done.1 = f32[2,256,512]{2,1,0:T(8,128)S(1)} collective-permute-done((f32[2,256,512]{2,1,0:T(8,128)S(1)}, f32[2,256,512]{2,1,0:T(8,128)S(1)}, u32[]{:S(2)}, u32[]{:S(2)}) %collective-permute-start.1) | collective-permute-done | bytes 1048608 | tf_op jit(solution)/shard_map/while/body/eval_jaxpr/ppermute | solution.py:16
  924.9 6.8 collective-permute-start.1
  931.7 15.1 %collective-permute-done.1 = f32[2,256,512]{2,1,0:T(8,128)S(1)} collective-permute-done((f32[2,256,512]{2,1,0:T(8,128)S(1)}, f32[2,256,512]{2,1,0:T(8,128)S(1)}, u32[]{:S(2)}, u32[]{:S(2)}) %collective-permute-start.1) | collective-permute-done | bytes 1048608 | tf_op jit(solution)/shard_map/while/body/eval_jaxpr/ppermute | solution.py:16
  948.3 6.8 collective-permute-start.1
  955.0 15.1 %collective-permute-done.1 = f32[2,256,512]{2,1,0:T(8,128)S(1)} collective-permute-done((f32[2,256,512]{2,1,0:T(8,128)S(1)}, f32[2,256,512]{2,1,0:T(8,128)S(1)}, u32[]{:S(2)}, u32[]{:S(2)}) %collective-permute-start.1) | collective-permute-done | bytes 1048608 | tf_op jit(solution)/shard_map/while/body/eval_jaxpr/ppermute | solution.py:16
  971.6 6.8 collective-permute-start.1
  978.4 15.1 %collective-permute-done.1 = f32[2,256,512]{2,1,0:T(8,128)S(1)} collective-permute-done((f32[2,256,512]{2,1,0:T(8,128)S(1)}, f32[2,256,512]{2,1,0:T(8,128)S(1)}, u32[]{:S(2)}, u32[]{:S(2)}) %collective-permute-start.1) | collective-permute-done | bytes 1048608 | tf_op jit(solution)/shard_map/while/body/eval_jaxpr/ppermute | solution.py:16
  994.9 6.8 collective-permute-start.1
  1001.7 16.0 %collective-permute-done.1 = f32[2,256,512]{2,1,0:T(8,128)S(1)} collective-permute-done((f32[2,256,512]{2,1,0:T(8,128)S(1)}, f32[2,256,512]{2,1,0:T(8,128)S(1)}, u32[]{:S(2)}, u32[]{:S(2)}) %collective-permute-start.1) | collective-permute-done | bytes 1048608 | tf_op jit(solution)/shard_map/while/body/eval_jaxpr/ppermute | solution.py:16
  1019.1 6.8 collective-permute-start.1
  1025.9 17.1 %collective-permute-done.1 = f32[2,256,512]{2,1,0:T(8,128)S(1)} collective-permute-done((f32[2,256,512]{2,1,0:T(8,128)S(1)}, f32[2,256,512]{2,1,0:T(8,128)S(1)}, u32[]{:S(2)}, u32[]{:S(2)}) %collective-permute-start.1) | collective-permute-done | bytes 1048608 | tf_op jit(solution)/shard_map/while/body/eval_jaxpr/ppermute | solution.py:16
  1044.4 6.8 collective-permute-start.1
  1051.2 18.1 %collective-permute-done.1 = f32[2,256,512]{2,1,0:T(8,128)S(1)} collective-permute-done((f32[2,256,512]{2,1,0:T(8,128)S(1)}, f32[2,256,512]{2,1,0:T(8,128)S(1)}, u32[]{:S(2)}, u32[]{:S(2)}) %collective-permute-start.1) | collective-permute-done | bytes 1048608 | tf_op jit(solution)/shard_map/while/body/eval_jaxpr/ppermute | solution.py:16
  1070.7 6.8 collective-permute-start.1
  1077.5 12.3 %collective-permute-done.1 = f32[2,256,512]{2,1,0:T(8,128)S(1)} collective-permute-done((f32[2,256,512]{2,1,0:T(8,128)S(1)}, f32[2,256,512]{2,1,0:T(8,128)S(1)}, u32[]{:S(2)}, u32[]{:S(2)}) %collective-permute-start.1) | collective-permute-done | bytes 1048608 | tf_op jit(solution)/shard_map/while/body/eval_jaxpr/ppermute | solution.py:16
  (286 shorter events, 252.5 us)
Async XLA Ops:
  0.6 10.1 copy-start.19
  2.6 14.6 %collective-permute-start.2 = (bf16[2,256,512]{2,1,0:T(8,128)(2,1)}, bf16[2,256,512]{2,1,0:T(8,128)(2,1)}, u32[]{:S(2)}, u32[]{:S(2)}) collective-permute-start(bf16[2,256,512]{2,1,0:T(8,128)(2,1)} %pad_maximum_fusion.2), channel_id=1, source_target_pairs={{32,0},{36,4},{40,8},{44,12},{48,16},{52,20},{56,24},{60,28},{64,3... | collective-permute-start | bytes 1572872 | tf_op jit(solution)/shard_map/ppermute | solution.py:16
  22.7 18.5 %collective-permute-start = (bf16[2,256,512]{2,1,0:T(8,128)(2,1)}, bf16[2,256,512]{2,1,0:T(8,128)(2,1)S(1)}, u32[]{:S(2)}, u32[]{:S(2)}) collective-permute-start(bf16[2,256,512]{2,1,0:T(8,128)(2,1)} %get-tuple-element.288), channel_id=1, source_target_pairs={{124,0},{0,4},{4,8},{8,12},{12,16},{16,20},{20,24},{24,28},{28,32}... | collective-permute-start | bytes 1572872 | tf_op jit(solution)/shard_map/while/body/eval_jaxpr/ppermute | solution.py:16
  42.9 16.6 %collective-permute-start = (bf16[2,256,512]{2,1,0:T(8,128)(2,1)}, bf16[2,256,512]{2,1,0:T(8,128)(2,1)S(1)}, u32[]{:S(2)}, u32[]{:S(2)}) collective-permute-start(bf16[2,256,512]{2,1,0:T(8,128)(2,1)} %get-tuple-element.288), channel_id=1, source_target_pairs={{124,0},{0,4},{4,8},{8,12},{12,16},{16,20},{20,24},{24,28},{28,32}... | collective-permute-start | bytes 1572872 | tf_op jit(solution)/shard_map/while/body/eval_jaxpr/ppermute | solution.py:16
  61.2 15.7 %collective-permute-start = (bf16[2,256,512]{2,1,0:T(8,128)(2,1)}, bf16[2,256,512]{2,1,0:T(8,128)(2,1)S(1)}, u32[]{:S(2)}, u32[]{:S(2)}) collective-permute-start(bf16[2,256,512]{2,1,0:T(8,128)(2,1)} %get-tuple-element.288), channel_id=1, source_target_pairs={{124,0},{0,4},{4,8},{8,12},{12,16},{16,20},{20,24},{24,28},{28,32}... | collective-permute-start | bytes 1572872 | tf_op jit(solution)/shard_map/while/body/eval_jaxpr/ppermute | solution.py:16
  78.5 14.7 %collective-permute-start = (bf16[2,256,512]{2,1,0:T(8,128)(2,1)}, bf16[2,256,512]{2,1,0:T(8,128)(2,1)S(1)}, u32[]{:S(2)}, u32[]{:S(2)}) collective-permute-start(bf16[2,256,512]{2,1,0:T(8,128)(2,1)} %get-tuple-element.288), channel_id=1, source_target_pairs={{124,0},{0,4},{4,8},{8,12},{12,16},{16,20},{20,24},{24,28},{28,32}... | collective-permute-start | bytes 1572872 | tf_op jit(solution)/shard_map/while/body/eval_jaxpr/ppermute | solution.py:16
  94.8 13.8 %collective-permute-start = (bf16[2,256,512]{2,1,0:T(8,128)(2,1)}, bf16[2,256,512]{2,1,0:T(8,128)(2,1)S(1)}, u32[]{:S(2)}, u32[]{:S(2)}) collective-permute-start(bf16[2,256,512]{2,1,0:T(8,128)(2,1)} %get-tuple-element.288), channel_id=1, source_target_pairs={{124,0},{0,4},{4,8},{8,12},{12,16},{16,20},{20,24},{24,28},{28,32}... | collective-permute-start | bytes 1572872 | tf_op jit(solution)/shard_map/while/body/eval_jaxpr/ppermute | solution.py:16
  110.3 13.6 %collective-permute-start = (bf16[2,256,512]{2,1,0:T(8,128)(2,1)}, bf16[2,256,512]{2,1,0:T(8,128)(2,1)S(1)}, u32[]{:S(2)}, u32[]{:S(2)}) collective-permute-start(bf16[2,256,512]{2,1,0:T(8,128)(2,1)} %get-tuple-element.288), channel_id=1, source_target_pairs={{124,0},{0,4},{4,8},{8,12},{12,16},{16,20},{20,24},{24,28},{28,32}... | collective-permute-start | bytes 1572872 | tf_op jit(solution)/shard_map/while/body/eval_jaxpr/ppermute | solution.py:16
  125.6 13.6 %collective-permute-start = (bf16[2,256,512]{2,1,0:T(8,128)(2,1)}, bf16[2,256,512]{2,1,0:T(8,128)(2,1)S(1)}, u32[]{:S(2)}, u32[]{:S(2)}) collective-permute-start(bf16[2,256,512]{2,1,0:T(8,128)(2,1)} %get-tuple-element.288), channel_id=1, source_target_pairs={{124,0},{0,4},{4,8},{8,12},{12,16},{16,20},{20,24},{24,28},{28,32}... | collective-permute-start | bytes 1572872 | tf_op jit(solution)/shard_map/while/body/eval_jaxpr/ppermute | solution.py:16
  140.9 13.7 %collective-permute-start = (bf16[2,256,512]{2,1,0:T(8,128)(2,1)}, bf16[2,256,512]{2,1,0:T(8,128)(2,1)S(1)}, u32[]{:S(2)}, u32[]{:S(2)}) collective-permute-start(bf16[2,256,512]{2,1,0:T(8,128)(2,1)} %get-tuple-element.288), channel_id=1, source_target_pairs={{124,0},{0,4},{4,8},{8,12},{12,16},{16,20},{20,24},{24,28},{28,32}... | collective-permute-start | bytes 1572872 | tf_op jit(solution)/shard_map/while/body/eval_jaxpr/ppermute | solution.py:16
  156.2 14.8 %collective-permute-start = (bf16[2,256,512]{2,1,0:T(8,128)(2,1)}, bf16[2,256,512]{2,1,0:T(8,128)(2,1)S(1)}, u32[]{:S(2)}, u32[]{:S(2)}) collective-permute-start(bf16[2,256,512]{2,1,0:T(8,128)(2,1)} %get-tuple-element.288), channel_id=1, source_target_pairs={{124,0},{0,4},{4,8},{8,12},{12,16},{16,20},{20,24},{24,28},{28,32}... | collective-permute-start | bytes 1572872 | tf_op jit(solution)/shard_map/while/body/eval_jaxpr/ppermute | solution.py:16
  172.6 15.8 %collective-permute-start = (bf16[2,256,512]{2,1,0:T(8,128)(2,1)}, bf16[2,256,512]{2,1,0:T(8,128)(2,1)S(1)}, u32[]{:S(2)}, u32[]{:S(2)}) collective-permute-start(bf16[2,256,512]{2,1,0:T(8,128)(2,1)} %get-tuple-element.288), channel_id=1, source_target_pairs={{124,0},{0,4},{4,8},{8,12},{12,16},{16,20},{20,24},{24,28},{28,32}... | collective-permute-start | bytes 1572872 | tf_op jit(solution)/shard_map/while/body/eval_jaxpr/ppermute | solution.py:16
  190.1 16.9 %collective-permute-start = (bf16[2,256,512]{2,1,0:T(8,128)(2,1)}, bf16[2,256,512]{2,1,0:T(8,128)(2,1)S(1)}, u32[]{:S(2)}, u32[]{:S(2)}) collective-permute-start(bf16[2,256,512]{2,1,0:T(8,128)(2,1)} %get-tuple-element.288), channel_id=1, source_target_pairs={{124,0},{0,4},{4,8},{8,12},{12,16},{16,20},{20,24},{24,28},{28,32}... | collective-permute-start | bytes 1572872 | tf_op jit(solution)/shard_map/while/body/eval_jaxpr/ppermute | solution.py:16
  208.7 18.1 %collective-permute-start = (bf16[2,256,512]{2,1,0:T(8,128)(2,1)}, bf16[2,256,512]{2,1,0:T(8,128)(2,1)S(1)}, u32[]{:S(2)}, u32[]{:S(2)}) collective-permute-start(bf16[2,256,512]{2,1,0:T(8,128)(2,1)} %get-tuple-element.288), channel_id=1, source_target_pairs={{124,0},{0,4},{4,8},{8,12},{12,16},{16,20},{20,24},{24,28},{28,32}... | collective-permute-start | bytes 1572872 | tf_op jit(solution)/shard_map/while/body/eval_jaxpr/ppermute | solution.py:16
  228.4 19.2 %collective-permute-start = (bf16[2,256,512]{2,1,0:T(8,128)(2,1)}, bf16[2,256,512]{2,1,0:T(8,128)(2,1)S(1)}, u32[]{:S(2)}, u32[]{:S(2)}) collective-permute-start(bf16[2,256,512]{2,1,0:T(8,128)(2,1)} %get-tuple-element.288), channel_id=1, source_target_pairs={{124,0},{0,4},{4,8},{8,12},{12,16},{16,20},{20,24},{24,28},{28,32}... | collective-permute-start | bytes 1572872 | tf_op jit(solution)/shard_map/while/body/eval_jaxpr/ppermute | solution.py:16
  249.3 18.4 %collective-permute-start = (bf16[2,256,512]{2,1,0:T(8,128)(2,1)}, bf16[2,256,512]{2,1,0:T(8,128)(2,1)S(1)}, u32[]{:S(2)}, u32[]{:S(2)}) collective-permute-start(bf16[2,256,512]{2,1,0:T(8,128)(2,1)} %get-tuple-element.288), channel_id=1, source_target_pairs={{124,0},{0,4},{4,8},{8,12},{12,16},{16,20},{20,24},{24,28},{28,32}... | collective-permute-start | bytes 1572872 | tf_op jit(solution)/shard_map/while/body/eval_jaxpr/ppermute | solution.py:16
  269.3 17.5 %collective-permute-start = (bf16[2,256,512]{2,1,0:T(8,128)(2,1)}, bf16[2,256,512]{2,1,0:T(8,128)(2,1)S(1)}, u32[]{:S(2)}, u32[]{:S(2)}) collective-permute-start(bf16[2,256,512]{2,1,0:T(8,128)(2,1)} %get-tuple-element.288), channel_id=1, source_target_pairs={{124,0},{0,4},{4,8},{8,12},{12,16},{16,20},{20,24},{24,28},{28,32}... | collective-permute-start | bytes 1572872 | tf_op jit(solution)/shard_map/while/body/eval_jaxpr/ppermute | solution.py:16
  288.5 13.6 %collective-permute-start = (bf16[2,256,512]{2,1,0:T(8,128)(2,1)}, bf16[2,256,512]{2,1,0:T(8,128)(2,1)S(1)}, u32[]{:S(2)}, u32[]{:S(2)}) collective-permute-start(bf16[2,256,512]{2,1,0:T(8,128)(2,1)} %get-tuple-element.288), channel_id=1, source_target_pairs={{124,0},{0,4},{4,8},{8,12},{12,16},{16,20},{20,24},{24,28},{28,32}... | collective-permute-start | bytes 1572872 | tf_op jit(solution)/shard_map/while/body/eval_jaxpr/ppermute | solution.py:16
  357.0 4.9 copy-start.14
  366.6 9.2 slice-start.6
  366.6 9.2 slice-start.12
  366.6 9.2 slice-start.7
  366.6 9.2 slice-start.13
  390.8 4.9 copy-start.13
  400.5 9.2 slice-start.8
  400.5 9.2 slice-start.14
  400.5 9.2 slice-start.9
  400.5 9.2 slice-start.15
  424.9 4.9 copy-start.12
  434.6 9.2 slice-start.10
  434.6 9.2 slice-start.16
  434.6 9.2 slice-start.11
  434.6 9.2 slice-start.17
  438.3 4.1 copy-start.10
  497.0 4.5 copy-start.5
  497.0 4.5 copy-start.6
  497.0 5.6 copy-start.11
  506.5 8.4 copy-start.15
  511.3 6.7 slice-start.4
  511.3 6.7 slice-start.18
  511.3 7.0 slice-start.5
  511.3 7.8 slice-start.19
  609.4 8.0 copy-start.27
  628.2 5.9 slice-start
  686.7 25.4 %collective-permute-start.1 = (f32[2,256,512]{2,1,0:T(8,128)S(1)}, f32[2,256,512]{2,1,0:T(8,128)S(1)}, u32[]{:S(2)}, u32[]{:S(2)}) collective-permute-start(f32[2,256,512]{2,1,0:T(8,128)S(1)} %get-tuple-element.308), channel_id=1, source_target_pairs={{4,0},{8,4},{12,8},{16,12},{20,16},{24,20},{28,24},{32,28},{36,32}... | collective-permute-start | bytes 3145736 | tf_op jit(solution)/shard_map/while/body/eval_jaxpr/ppermute | solution.py:16
  713.5 27.4 %collective-permute-start.1 = (f32[2,256,512]{2,1,0:T(8,128)S(1)}, f32[2,256,512]{2,1,0:T(8,128)S(1)}, u32[]{:S(2)}, u32[]{:S(2)}) collective-permute-start(f32[2,256,512]{2,1,0:T(8,128)S(1)} %get-tuple-element.308), channel_id=1, source_target_pairs={{4,0},{8,4},{12,8},{16,12},{20,16},{24,20},{28,24},{32,28},{36,32}... | collective-permute-start | bytes 3145736 | tf_op jit(solution)/shard_map/while/body/eval_jaxpr/ppermute | solution.py:16
  742.4 27.4 %collective-permute-start.1 = (f32[2,256,512]{2,1,0:T(8,128)S(1)}, f32[2,256,512]{2,1,0:T(8,128)S(1)}, u32[]{:S(2)}, u32[]{:S(2)}) collective-permute-start(f32[2,256,512]{2,1,0:T(8,128)S(1)} %get-tuple-element.308), channel_id=1, source_target_pairs={{4,0},{8,4},{12,8},{16,12},{20,16},{24,20},{28,24},{32,28},{36,32}... | collective-permute-start | bytes 3145736 | tf_op jit(solution)/shard_map/while/body/eval_jaxpr/ppermute | solution.py:16
  771.2 26.5 %collective-permute-start.1 = (f32[2,256,512]{2,1,0:T(8,128)S(1)}, f32[2,256,512]{2,1,0:T(8,128)S(1)}, u32[]{:S(2)}, u32[]{:S(2)}) collective-permute-start(f32[2,256,512]{2,1,0:T(8,128)S(1)} %get-tuple-element.308), channel_id=1, source_target_pairs={{4,0},{8,4},{12,8},{16,12},{20,16},{24,20},{28,24},{32,28},{36,32}... | collective-permute-start | bytes 3145736 | tf_op jit(solution)/shard_map/while/body/eval_jaxpr/ppermute | solution.py:16
  799.1 25.6 %collective-permute-start.1 = (f32[2,256,512]{2,1,0:T(8,128)S(1)}, f32[2,256,512]{2,1,0:T(8,128)S(1)}, u32[]{:S(2)}, u32[]{:S(2)}) collective-permute-start(f32[2,256,512]{2,1,0:T(8,128)S(1)} %get-tuple-element.308), channel_id=1, source_target_pairs={{4,0},{8,4},{12,8},{16,12},{20,16},{24,20},{28,24},{32,28},{36,32}... | collective-permute-start | bytes 3145736 | tf_op jit(solution)/shard_map/while/body/eval_jaxpr/ppermute | solution.py:16
  826.1 24.6 %collective-permute-start.1 = (f32[2,256,512]{2,1,0:T(8,128)S(1)}, f32[2,256,512]{2,1,0:T(8,128)S(1)}, u32[]{:S(2)}, u32[]{:S(2)}) collective-permute-start(f32[2,256,512]{2,1,0:T(8,128)S(1)} %get-tuple-element.308), channel_id=1, source_target_pairs={{4,0},{8,4},{12,8},{16,12},{20,16},{24,20},{28,24},{32,28},{36,32}... | collective-permute-start | bytes 3145736 | tf_op jit(solution)/shard_map/while/body/eval_jaxpr/ppermute | solution.py:16
  852.2 23.7 %collective-permute-start.1 = (f32[2,256,512]{2,1,0:T(8,128)S(1)}, f32[2,256,512]{2,1,0:T(8,128)S(1)}, u32[]{:S(2)}, u32[]{:S(2)}) collective-permute-start(f32[2,256,512]{2,1,0:T(8,128)S(1)} %get-tuple-element.308), channel_id=1, source_target_pairs={{4,0},{8,4},{12,8},{16,12},{20,16},{24,20},{28,24},{32,28},{36,32}... | collective-permute-start | bytes 3145736 | tf_op jit(solution)/shard_map/while/body/eval_jaxpr/ppermute | solution.py:16
  877.4 22.8 %collective-permute-start.1 = (f32[2,256,512]{2,1,0:T(8,128)S(1)}, f32[2,256,512]{2,1,0:T(8,128)S(1)}, u32[]{:S(2)}, u32[]{:S(2)}) collective-permute-start(f32[2,256,512]{2,1,0:T(8,128)S(1)} %get-tuple-element.308), channel_id=1, source_target_pairs={{4,0},{8,4},{12,8},{16,12},{20,16},{24,20},{28,24},{32,28},{36,32}... | collective-permute-start | bytes 3145736 | tf_op jit(solution)/shard_map/while/body/eval_jaxpr/ppermute | solution.py:16
  901.6 21.9 %collective-permute-start.1 = (f32[2,256,512]{2,1,0:T(8,128)S(1)}, f32[2,256,512]{2,1,0:T(8,128)S(1)}, u32[]{:S(2)}, u32[]{:S(2)}) collective-permute-start(f32[2,256,512]{2,1,0:T(8,128)S(1)} %get-tuple-element.308), channel_id=1, source_target_pairs={{4,0},{8,4},{12,8},{16,12},{20,16},{24,20},{28,24},{32,28},{36,32}... | collective-permute-start | bytes 3145736 | tf_op jit(solution)/shard_map/while/body/eval_jaxpr/ppermute | solution.py:16
  924.9 21.9 %collective-permute-start.1 = (f32[2,256,512]{2,1,0:T(8,128)S(1)}, f32[2,256,512]{2,1,0:T(8,128)S(1)}, u32[]{:S(2)}, u32[]{:S(2)}) collective-permute-start(f32[2,256,512]{2,1,0:T(8,128)S(1)} %get-tuple-element.308), channel_id=1, source_target_pairs={{4,0},{8,4},{12,8},{16,12},{20,16},{24,20},{28,24},{32,28},{36,32}... | collective-permute-start | bytes 3145736 | tf_op jit(solution)/shard_map/while/body/eval_jaxpr/ppermute | solution.py:16
  948.3 21.9 %collective-permute-start.1 = (f32[2,256,512]{2,1,0:T(8,128)S(1)}, f32[2,256,512]{2,1,0:T(8,128)S(1)}, u32[]{:S(2)}, u32[]{:S(2)}) collective-permute-start(f32[2,256,512]{2,1,0:T(8,128)S(1)} %get-tuple-element.308), channel_id=1, source_target_pairs={{4,0},{8,4},{12,8},{16,12},{20,16},{24,20},{28,24},{32,28},{36,32}... | collective-permute-start | bytes 3145736 | tf_op jit(solution)/shard_map/while/body/eval_jaxpr/ppermute | solution.py:16
  971.6 21.9 %collective-permute-start.1 = (f32[2,256,512]{2,1,0:T(8,128)S(1)}, f32[2,256,512]{2,1,0:T(8,128)S(1)}, u32[]{:S(2)}, u32[]{:S(2)}) collective-permute-start(f32[2,256,512]{2,1,0:T(8,128)S(1)} %get-tuple-element.308), channel_id=1, source_target_pairs={{4,0},{8,4},{12,8},{16,12},{20,16},{24,20},{28,24},{32,28},{36,32}... | collective-permute-start | bytes 3145736 | tf_op jit(solution)/shard_map/while/body/eval_jaxpr/ppermute | solution.py:16
  994.9 22.7 %collective-permute-start.1 = (f32[2,256,512]{2,1,0:T(8,128)S(1)}, f32[2,256,512]{2,1,0:T(8,128)S(1)}, u32[]{:S(2)}, u32[]{:S(2)}) collective-permute-start(f32[2,256,512]{2,1,0:T(8,128)S(1)} %get-tuple-element.308), channel_id=1, source_target_pairs={{4,0},{8,4},{12,8},{16,12},{20,16},{24,20},{28,24},{32,28},{36,32}... | collective-permute-start | bytes 3145736 | tf_op jit(solution)/shard_map/while/body/eval_jaxpr/ppermute | solution.py:16
  1019.1 23.8 %collective-permute-start.1 = (f32[2,256,512]{2,1,0:T(8,128)S(1)}, f32[2,256,512]{2,1,0:T(8,128)S(1)}, u32[]{:S(2)}, u32[]{:S(2)}) collective-permute-start(f32[2,256,512]{2,1,0:T(8,128)S(1)} %get-tuple-element.308), channel_id=1, source_target_pairs={{4,0},{8,4},{12,8},{16,12},{20,16},{24,20},{28,24},{32,28},{36,32}... | collective-permute-start | bytes 3145736 | tf_op jit(solution)/shard_map/while/body/eval_jaxpr/ppermute | solution.py:16
  1044.4 24.9 %collective-permute-start.1 = (f32[2,256,512]{2,1,0:T(8,128)S(1)}, f32[2,256,512]{2,1,0:T(8,128)S(1)}, u32[]{:S(2)}, u32[]{:S(2)}) collective-permute-start(f32[2,256,512]{2,1,0:T(8,128)S(1)} %get-tuple-element.308), channel_id=1, source_target_pairs={{4,0},{8,4},{12,8},{16,12},{20,16},{24,20},{28,24},{32,28},{36,32}... | collective-permute-start | bytes 3145736 | tf_op jit(solution)/shard_map/while/body/eval_jaxpr/ppermute | solution.py:16
  1070.7 19.1 %collective-permute-start.1 = (f32[2,256,512]{2,1,0:T(8,128)S(1)}, f32[2,256,512]{2,1,0:T(8,128)S(1)}, u32[]{:S(2)}, u32[]{:S(2)}) collective-permute-start(f32[2,256,512]{2,1,0:T(8,128)S(1)} %get-tuple-element.308), channel_id=1, source_target_pairs={{4,0},{8,4},{12,8},{16,12},{20,16},{24,20},{28,24},{32,28},{36,32}... | collective-permute-start | bytes 3145736 | tf_op jit(solution)/shard_map/while/body/eval_jaxpr/ppermute | solution.py:16
  1091.3 4.9 copy-start.20
  1091.3 4.9 copy-start.21
  1091.3 4.9 copy-start.22
  1092.2 10.9 collective-permute-start.3
  (18 other events, 51.9 us)
